TPU v7x, 32 devices: a whole 2x2x4 slice. The times are simulated.
32 devices in a mesh: site: 32 (over z, y, x, core).
Axes of the slice: x: 2, y: 2, z: 4, core: 2. Of those that a mesh axis runs over, the one named last changes fastest.
Arguments:
- sites: float32 [32, 2, 12, 128, 128], P('site'), may hold values from -0.5 to 0.5
- sector_sizes: int32 [32, 12], P('site'), may hold values from 64 to 128, as said below
- charge_steps: int32 [32], P('site'), may hold values from 0 to 1
- kept_counts: int32 [32, 12], P('site'), may hold values from 64 to 128, as said below
- gates: float32 [32, 6], P('site'), may hold values from 0.4 to 1.2
- sketches: float32 [32, 12, 256, 128], P('site'), may hold values from -0.375 to 0.375
Outputs:
- new_sites: float32 [32, 2, 12, 128, 128], P('site')
- totals: float32 [2], replicated
Inputs may be any that keep to these rules, and one draw needn't show every extreme that they name: `sector_sizes`: every sector holds at least 64 states; each bond has one sector of exactly 128 states. kept_counts[i, c] is at least 64 and at most sector_sizes[(i + 1) mod 32, c]; on each bond the sector of 128 states keeps all of them.
All inputs are finite; a program needn't handle non-finite values.
Results may differ from a plain program's by a relative error of at most 0.0003.
Values sent between devices are 32-bit elements; how exact they have to be, the bound alone decides.
A program may use at most 64 MiB of HBM per device.

v0:
```python
import jax
import jax.numpy as jnp
from jax import lax
from jax.sharding import PartitionSpec as P

STEPS = 4


def from_behind(value, axis, steps):
    count = lax.axis_size(axis)
    pairs = [(source, (source + steps) % count) for source in range(count)]
    return lax.ppermute(value, axis, pairs)


def shifted(value, axis, by):
    count = lax.axis_size(axis)
    pairs = [(i, i + by) for i in range(count) if 0 <= i + by < count]
    return lax.ppermute(value, axis, pairs)


def sector_index(count, shift, extra):
    return (jnp.arange(count, dtype=jnp.int32) + extra - shift) % count


def theta_blocks(left, right, shift, gate):
    count = left.shape[1]
    lower_mid = sector_index(count, shift, 0)
    upper_mid = sector_index(count, shift, 1)

    def product(first, second):
        return jnp.einsum("lam,lmb->lab", first, second, precision=lax.Precision.HIGHEST)

    zero_zero = product(left[0], right[0][lower_mid])
    zero_one = product(left[0], right[1][lower_mid])
    one_zero = product(left[1], right[0][upper_mid])
    one_one = product(left[1], right[1][upper_mid])
    mixed_up = gate[2] * zero_one + gate[3] * one_zero
    mixed_down = gate[4] * zero_one + gate[5] * one_zero
    return (gate[0] * zero_zero, mixed_up, mixed_down, gate[1] * one_one)


def split_sectors(blocks, middle, shift, sketch, kept):
    count = blocks[0].shape[0]
    width = blocks[0].shape[-1]
    top = (middle + shift) % count
    bottom = (middle + shift - 1) % count
    upper = jnp.concatenate([blocks[0][top], blocks[1][top]], axis=2)
    lower = jnp.concatenate([blocks[2][bottom], blocks[3][bottom]], axis=2)
    matrix = jnp.concatenate([upper, lower], axis=1)
    used = (jnp.arange(width, dtype=jnp.int32)[None, :] < kept[:, None]).astype(jnp.float32)
    sample = jnp.einsum(
        "kij,kjs->kis", matrix, sketch * used[:, None, :], precision=lax.Precision.HIGHEST
    )
    gram = jnp.einsum("kis,kit->kst", sample, sample, precision=lax.Precision.HIGHEST)
    diag_sum = jnp.sum(sample * sample, axis=(1, 2))
    ridge = 0.001 * diag_sum / kept.astype(jnp.float32) + 1e-06
    identity = jnp.eye(width, dtype=jnp.float32)[None]
    gram = gram + identity * ridge[:, None, None] + identity * (1.0 - used)[:, None, :]
    factor = jnp.linalg.cholesky(gram)
    solved = jax.scipy.linalg.solve_triangular(factor, jnp.swapaxes(sample, 1, 2), lower=True)
    basis = jnp.swapaxes(solved, 1, 2)
    reduced = jnp.einsum("kis,kij->ksj", basis, matrix, precision=lax.Precision.HIGHEST)
    return (basis, reduced, jnp.sum(matrix * matrix), jnp.sum(reduced * reduced))


def rebuild_left(basis, shift):
    count = basis.shape[0]
    width = basis.shape[2]
    return jnp.stack(
        [basis[sector_index(count, shift, 0), :width], basis[sector_index(count, shift, 1), width:]]
    )


def rebuild_right(reduced, weight):
    width = reduced.shape[1]
    return jnp.stack([reduced[..., :width], reduced[..., width:]]) / jnp.sqrt(weight)


def mask_tensor(tensor, sizes, next_sizes, step):
    count = tensor.shape[1]
    width = tensor.shape[-1]
    states = jnp.arange(width, dtype=jnp.int32)
    rows = states[None, :] < sizes[:, None]
    masks = []
    for phys in range(2):
        target = sector_index(count, step, phys)
        cols = states[None, :] < next_sizes[target][:, None]
        masks.append(rows[:, :, None] & cols[:, None, :])
    return tensor * jnp.stack(masks).astype(jnp.float32)


def body(sites, sector_sizes, charge_steps, kept_counts, gates, sketches):
    tensor = sites[0]
    step = charge_steps[0]
    kept = kept_counts[0]
    gate = gates[0]
    sketch = sketches[0]
    position = lax.axis_index("site")
    chain = lax.axis_size("site")
    next_sizes = from_behind(sector_sizes, "site", -1)[0]
    tensor = mask_tensor(tensor, sector_sizes[0], next_sizes, step)
    count = tensor.shape[1]
    prev_gates, prev_sketches = shifted((gates, sketches), "site", 1)
    prev_steps, prev_kept = shifted((charge_steps, kept_counts), "site", 1)

    def one_sweep(tensor, lost_sum, log_sum, parity):
        is_left = (position % 2 == parity) & (position + 1 < chain)
        is_right = ((position - 1) % 2 == parity) & (position >= 1)
        from_right = shifted(tensor, "site", -1)
        from_left = shifted(tensor, "site", 1)
        left_in = jnp.where(is_left, tensor, from_left)
        right_in = jnp.where(is_left, from_right, tensor)
        shift_in = jnp.where(is_left, step, prev_steps[0])
        gate_in = jnp.where(is_left, gate, prev_gates[0])
        sketch_in = jnp.where(is_left, sketch, prev_sketches[0])
        kept_in = jnp.where(is_left, kept, prev_kept[0])
        blocks = theta_blocks(left_in, right_in, shift_in, gate_in)
        half = count // 2
        middle = jnp.arange(half, dtype=jnp.int32) + jnp.where(is_left, 0, half)
        basis_half, reduced_half, total_half, weight_half = split_sectors(
            blocks, middle, shift_in, sketch_in[middle], kept_in[middle]
        )
        partial_value = jnp.stack([total_half, weight_half])
        basis_other, sums_right = shifted((basis_half, partial_value), "site", -1)
        reduced_other, sums_left = shifted((reduced_half, partial_value), "site", 1)
        basis = jnp.concatenate([basis_half, basis_other], axis=0)
        reduced = jnp.concatenate([reduced_other, reduced_half], axis=0)
        total = total_half + sums_right[0]
        weight_left = weight_half + sums_right[1]
        weight_right = weight_half + sums_left[1]
        new_left = rebuild_left(basis, shift_in)
        new_right = rebuild_right(reduced, weight_right)
        lost = 1.0 - weight_left / total
        log_norm = jnp.log(total)
        tensor = jnp.where(is_left, new_left, jnp.where(is_right, new_right, tensor))
        lost_now = jnp.where(is_left, lost, 0.0)
        log_now = jnp.where(is_left, log_norm, 0.0)
        summed = lax.psum((lost_now, log_now), "site")
        lost_sum = lost_sum + summed[0]
        log_sum = log_sum + summed[1]
        return (tensor, lost_sum, log_sum)

    def one_step(index, carry):
        tensor, lost_sum, log_sum = carry
        tensor, lost_sum, log_sum = one_sweep(tensor, lost_sum, log_sum, 0)
        tensor, lost_sum, log_sum = one_sweep(tensor, lost_sum, log_sum, 1)
        return (tensor, lost_sum, log_sum)

    start = (tensor, jnp.zeros((), jnp.float32), jnp.zeros((), jnp.float32))
    tensor, lost_sum, log_sum = lax.fori_loop(0, STEPS, one_step, start)
    return (tensor[None], jnp.stack([lost_sum, log_sum]))


def solution(mesh):
    placed = (
        P("site", None, None, None, None),
        P("site", None),
        P("site"),
        P("site", None),
        P("site", None),
        P("site", None, None, None),
    )
    return jax.shard_map(
        body,
        mesh=mesh,
        in_specs=placed,
        out_specs=(P("site", None, None, None, None), P()),
        check_vma=False,
    )
```

profile of v0, /device:TPU:0, one launch (start us, length us, event | category | flops | bytes accessed | tf_op | source)
XLA Modules:
  0.0 2202.5 jit_solution(7579148060066453691)
XLA Ops:
  29.4 2171.8 %while.19 = (s32[]{:T(128)}, f32[2,12,128,128]{3,2,1,0:T(8,128)S(1)}, f32[]{:T(128)}, f32[]{:T(128)}, pred[]{:T(512)}, /*index=5*/f32[1,6]{1,0:T(1,128)S(1)}, f3...) while((s32[]{:T(128)}, ...), condition=%wide.region_13.16_spmd, body=%wide.region_0.15_spmd.sunk | while | flops 6066817024 | bytes 249431616 | solution.py:150
  78.6 70.7 %custom-call.108 = f32[6,128,128]{2,1,0:T(8,128)S(1)} custom-call(f32[6,128,128]{2,1,0:T(8,128)S(1)} %fusion.138), custom_call_target="Cholesky" | custom-call | tf_op jit(solution)/shard_map/while/body/eval_jaxpr/jit(cholesky)/cholesky | solution.py:59
  150.3 59.0 %custom-call.109 = f32[6,1,128,128]{2,3,1,0:T(8,128)S(1)} custom-call(f32[6,1,128,128]{3,2,1,0:T(8,128)S(1)} %select_bitcast_fusion.6), custom_call_target="InvertDiagBlocksLowerTriangular" | custom-call | tf_op jit(solution)/shard_map/while/body/eval_jaxpr/jit(_solve_triangular)/vmap()/triangular_solve | solution.py:60
  318.6 70.5 %custom-call.110 = f32[6,128,128]{2,1,0:T(8,128)S(1)} custom-call(f32[6,128,128]{2,1,0:T(8,128)S(1)} %fusion.146), custom_call_target="Cholesky" | custom-call | tf_op jit(solution)/shard_map/while/body/eval_jaxpr/jit(cholesky)/cholesky | solution.py:59
  390.2 59.0 %custom-call.111 = f32[6,1,128,128]{2,3,1,0:T(8,128)S(1)} custom-call(f32[6,1,128,128]{3,2,1,0:T(8,128)S(1)} %select_bitcast_fusion.7), custom_call_target="InvertDiagBlocksLowerTriangular" | custom-call | tf_op jit(solution)/shard_map/while/body/eval_jaxpr/jit(_solve_triangular)/vmap()/triangular_solve | solution.py:60
  453.9 36.7 %collective-permute-start.8 = (f32[6,128,256]{2,1,0:T(8,128)}, f32[6,128,256]{2,1,0:T(8,128)}, u32[]{:S(2)}, u32[]{:S(2)}) collective-permute-start(f32[6,128,256]{2,1,0:T(8,128)} %get-tuple-element.933), channel_id=1, source_target_pairs={{0,1},{1,2},{2,3},{3,4},{4,5},{5,6},{6,7},{7,8},{8,9},{9,10},{10,1... | collective-permute-start | bytes 2359304 | tf_op jit(solution)/shard_map/while/body/eval_jaxpr/ppermute | solution.py:18
  513.8 45.1 %all-reduce.6 = (f32[]{:T(128)}, f32[]{:T(128)}, f32[]{:T(128)}, f32[]{:T(128)}) all-reduce(f32[]{:T(128)S(6)} %select_n.941, f32[]{:T(128)S(6)} %select_n.942, f32[]{:T(128)S(6)} %select_n.943, f32[]{:T(128)S(6)} %select_n.944), channel_id=1, replica_groups=mesh['site'=32] {'site'}, use_global_device_ids=true, to_apply=%region_9.11 | all-reduce | flops 4 | bytes 32 | tf_op jit(solution)/shard_map/while/body/eval_jaxpr/psum | solution.py:138
  618.0 70.8 %custom-call.108 = f32[6,128,128]{2,1,0:T(8,128)S(1)} custom-call(f32[6,128,128]{2,1,0:T(8,128)S(1)} %fusion.138), custom_call_target="Cholesky" | custom-call | tf_op jit(solution)/shard_map/while/body/eval_jaxpr/jit(cholesky)/cholesky | solution.py:59
  689.9 59.0 %custom-call.109 = f32[6,1,128,128]{2,3,1,0:T(8,128)S(1)} custom-call(f32[6,1,128,128]{3,2,1,0:T(8,128)S(1)} %select_bitcast_fusion.6), custom_call_target="InvertDiagBlocksLowerTriangular" | custom-call | tf_op jit(solution)/shard_map/while/body/eval_jaxpr/jit(_solve_triangular)/vmap()/triangular_solve | solution.py:60
  857.3 70.6 %custom-call.110 = f32[6,128,128]{2,1,0:T(8,128)S(1)} custom-call(f32[6,128,128]{2,1,0:T(8,128)S(1)} %fusion.146), custom_call_target="Cholesky" | custom-call | tf_op jit(solution)/shard_map/while/body/eval_jaxpr/jit(cholesky)/cholesky | solution.py:59
  929.0 59.0 %custom-call.111 = f32[6,1,128,128]{2,3,1,0:T(8,128)S(1)} custom-call(f32[6,1,128,128]{3,2,1,0:T(8,128)S(1)} %select_bitcast_fusion.7), custom_call_target="InvertDiagBlocksLowerTriangular" | custom-call | tf_op jit(solution)/shard_map/while/body/eval_jaxpr/jit(_solve_triangular)/vmap()/triangular_solve | solution.py:60
  992.7 36.7 %collective-permute-start.8 = (f32[6,128,256]{2,1,0:T(8,128)}, f32[6,128,256]{2,1,0:T(8,128)}, u32[]{:S(2)}, u32[]{:S(2)}) collective-permute-start(f32[6,128,256]{2,1,0:T(8,128)} %get-tuple-element.933), channel_id=1, source_target_pairs={{0,1},{1,2},{2,3},{3,4},{4,5},{5,6},{6,7},{7,8},{8,9},{9,10},{10,1... | collective-permute-start | bytes 2359304 | tf_op jit(solution)/shard_map/while/body/eval_jaxpr/ppermute | solution.py:18
  1051.4 49.0 %all-reduce.6 = (f32[]{:T(128)}, f32[]{:T(128)}, f32[]{:T(128)}, f32[]{:T(128)}) all-reduce(f32[]{:T(128)S(6)} %select_n.941, f32[]{:T(128)S(6)} %select_n.942, f32[]{:T(128)S(6)} %select_n.943, f32[]{:T(128)S(6)} %select_n.944), channel_id=1, replica_groups=mesh['site'=32] {'site'}, use_global_device_ids=true, to_apply=%region_9.11 | all-reduce | flops 4 | bytes 32 | tf_op jit(solution)/shard_map/while/body/eval_jaxpr/psum | solution.py:138
  1159.4 70.6 %custom-call.108 = f32[6,128,128]{2,1,0:T(8,128)S(1)} custom-call(f32[6,128,128]{2,1,0:T(8,128)S(1)} %fusion.138), custom_call_target="Cholesky" | custom-call | tf_op jit(solution)/shard_map/while/body/eval_jaxpr/jit(cholesky)/cholesky | solution.py:59
  1231.1 59.0 %custom-call.109 = f32[6,1,128,128]{2,3,1,0:T(8,128)S(1)} custom-call(f32[6,1,128,128]{3,2,1,0:T(8,128)S(1)} %select_bitcast_fusion.6), custom_call_target="InvertDiagBlocksLowerTriangular" | custom-call | tf_op jit(solution)/shard_map/while/body/eval_jaxpr/jit(_solve_triangular)/vmap()/triangular_solve | solution.py:60
  1398.5 70.5 %custom-call.110 = f32[6,128,128]{2,1,0:T(8,128)S(1)} custom-call(f32[6,128,128]{2,1,0:T(8,128)S(1)} %fusion.146), custom_call_target="Cholesky" | custom-call | tf_op jit(solution)/shard_map/while/body/eval_jaxpr/jit(cholesky)/cholesky | solution.py:59
  1470.1 59.0 %custom-call.111 = f32[6,1,128,128]{2,3,1,0:T(8,128)S(1)} custom-call(f32[6,1,128,128]{3,2,1,0:T(8,128)S(1)} %select_bitcast_fusion.7), custom_call_target="InvertDiagBlocksLowerTriangular" | custom-call | tf_op jit(solution)/shard_map/while/body/eval_jaxpr/jit(_solve_triangular)/vmap()/triangular_solve | solution.py:60
  1592.5 47.8 %all-reduce.6 = (f32[]{:T(128)}, f32[]{:T(128)}, f32[]{:T(128)}, f32[]{:T(128)}) all-reduce(f32[]{:T(128)S(6)} %select_n.941, f32[]{:T(128)S(6)} %select_n.942, f32[]{:T(128)S(6)} %select_n.943, f32[]{:T(128)S(6)} %select_n.944), channel_id=1, replica_groups=mesh['site'=32] {'site'}, use_global_device_ids=true, to_apply=%region_9.11 | all-reduce | flops 4 | bytes 32 | tf_op jit(solution)/shard_map/while/body/eval_jaxpr/psum | solution.py:138
  1699.4 70.8 %custom-call.108 = f32[6,128,128]{2,1,0:T(8,128)S(1)} custom-call(f32[6,128,128]{2,1,0:T(8,128)S(1)} %fusion.138), custom_call_target="Cholesky" | custom-call | tf_op jit(solution)/shard_map/while/body/eval_jaxpr/jit(cholesky)/cholesky | solution.py:59
  1771.3 59.0 %custom-call.109 = f32[6,1,128,128]{2,3,1,0:T(8,128)S(1)} custom-call(f32[6,1,128,128]{3,2,1,0:T(8,128)S(1)} %select_bitcast_fusion.6), custom_call_target="InvertDiagBlocksLowerTriangular" | custom-call | tf_op jit(solution)/shard_map/while/body/eval_jaxpr/jit(_solve_triangular)/vmap()/triangular_solve | solution.py:60
  1938.7 70.6 %custom-call.110 = f32[6,128,128]{2,1,0:T(8,128)S(1)} custom-call(f32[6,128,128]{2,1,0:T(8,128)S(1)} %fusion.146), custom_call_target="Cholesky" | custom-call | tf_op jit(solution)/shard_map/while/body/eval_jaxpr/jit(cholesky)/cholesky | solution.py:59
  2010.4 59.0 %custom-call.111 = f32[6,1,128,128]{2,3,1,0:T(8,128)S(1)} custom-call(f32[6,1,128,128]{3,2,1,0:T(8,128)S(1)} %select_bitcast_fusion.7), custom_call_target="InvertDiagBlocksLowerTriangular" | custom-call | tf_op jit(solution)/shard_map/while/body/eval_jaxpr/jit(_solve_triangular)/vmap()/triangular_solve | solution.py:60
  2074.1 36.7 %collective-permute-start.8 = (f32[6,128,256]{2,1,0:T(8,128)}, f32[6,128,256]{2,1,0:T(8,128)}, u32[]{:S(2)}, u32[]{:S(2)}) collective-permute-start(f32[6,128,256]{2,1,0:T(8,128)} %get-tuple-element.933), channel_id=1, source_target_pairs={{0,1},{1,2},{2,3},{3,4},{4,5},{5,6},{6,7},{7,8},{8,9},{9,10},{10,1... | collective-permute-start | bytes 2359304 | tf_op jit(solution)/shard_map/while/body/eval_jaxpr/ppermute | solution.py:18
  2132.7 49.0 %all-reduce.6 = (f32[]{:T(128)}, f32[]{:T(128)}, f32[]{:T(128)}, f32[]{:T(128)}) all-reduce(f32[]{:T(128)S(6)} %select_n.941, f32[]{:T(128)S(6)} %select_n.942, f32[]{:T(128)S(6)} %select_n.943, f32[]{:T(128)S(6)} %select_n.944), channel_id=1, replica_groups=mesh['site'=32] {'site'}, use_global_device_ids=true, to_apply=%region_9.11 | all-reduce | flops 4 | bytes 32 | tf_op jit(solution)/shard_map/while/body/eval_jaxpr/psum | solution.py:138
  (802 shorter events, 814.8 us)
Async XLA Ops:
  0.6 20.4 collective-permute-start.16
  12.6 16.7 collective-permute-start.13
  29.4 16.6 collective-permute-start
  210.2 47.1 %collective-permute-start.2 = (f32[6,256,128]{1,2,0:T(8,128)S(1)}, f32[6,256,128]{1,2,0:T(8,128)S(1)}, u32[]{:S(2)}, u32[]{:S(2)}) collective-permute-start(f32[6,256,128]{1,2,0:T(8,128)S(1)} %bitcast.315), channel_id=1, source_target_pairs={{1,0},{2,1},{3,2},{4,3},{5,4},{6,5},{7,6},{8,7},{9,8},{10,9},{11,1... | collective-permute-start | bytes 2359304 | tf_op jit(solution)/shard_map/while/body/eval_jaxpr/ppermute | solution.py:18
  214.1 56.1 %collective-permute-start.3 = (f32[6,128,256]{2,1,0:T(8,128)}, f32[6,128,256]{2,1,0:T(8,128)}, u32[]{:S(2)}, u32[]{:S(2)}) collective-permute-start(f32[6,128,256]{2,1,0:T(8,128)} %get-tuple-element.909), channel_id=1, source_target_pairs={{0,1},{1,2},{2,3},{3,4},{4,5},{5,6},{6,7},{7,8},{8,9},{9,10},{10,1... | collective-permute-start | bytes 2359304 | tf_op jit(solution)/shard_map/while/body/eval_jaxpr/ppermute | solution.py:18
  272.7 11.8 collective-permute-start.5
  450.1 113.4 %collective-permute-start.7 = (f32[6,256,128]{1,2,0:T(8,128)S(1)}, f32[6,256,128]{1,2,0:T(8,128)S(1)}, u32[]{:S(2)}, u32[]{:S(2)}) collective-permute-start(f32[6,256,128]{1,2,0:T(8,128)S(1)} %bitcast.313), channel_id=1, source_target_pairs={{1,0},{2,1},{3,2},{4,3},{5,4},{6,5},{7,6},{8,7},{9,8},{10,9},{11,1... | collective-permute-start | bytes 2359304 | tf_op jit(solution)/shard_map/while/body/eval_jaxpr/ppermute | solution.py:18
  453.9 118.7 %collective-permute-start.8 = (f32[6,128,256]{2,1,0:T(8,128)}, f32[6,128,256]{2,1,0:T(8,128)}, u32[]{:S(2)}, u32[]{:S(2)}) collective-permute-start(f32[6,128,256]{2,1,0:T(8,128)} %get-tuple-element.933), channel_id=1, source_target_pairs={{0,1},{1,2},{2,3},{3,4},{4,5},{5,6},{6,7},{7,8},{8,9},{9,10},{10,1... | collective-permute-start | bytes 2359304 | tf_op jit(solution)/shard_map/while/body/eval_jaxpr/ppermute | solution.py:18
  509.6 49.4 %collective-permute-start.9 = (f32[2]{0:T(128)S(1)}, f32[2]{0:T(128)S(1)}, u32[]{:S(2)}, u32[]{:S(2)}) collective-permute-start(f32[2]{0:T(128)S(1)} %pad_maximum_fusion.14), channel_id=1, source_target_pairs={{0,1},{1,2},{2,3},{3,4},{4,5},{5,6},{6,7},{7,8},{8,9},{9,10},{10,1... | collective-permute-start | bytes 32 | tf_op jit(solution)/shard_map/while/body/eval_jaxpr/ppermute | solution.py:18
  749.8 46.4 %collective-permute-start.2 = (f32[6,256,128]{1,2,0:T(8,128)S(1)}, f32[6,256,128]{1,2,0:T(8,128)S(1)}, u32[]{:S(2)}, u32[]{:S(2)}) collective-permute-start(f32[6,256,128]{1,2,0:T(8,128)S(1)} %bitcast.315), channel_id=1, source_target_pairs={{1,0},{2,1},{3,2},{4,3},{5,4},{6,5},{7,6},{8,7},{9,8},{10,9},{11,1... | collective-permute-start | bytes 2359304 | tf_op jit(solution)/shard_map/while/body/eval_jaxpr/ppermute | solution.py:18
  753.7 55.2 %collective-permute-start.3 = (f32[6,128,256]{2,1,0:T(8,128)}, f32[6,128,256]{2,1,0:T(8,128)}, u32[]{:S(2)}, u32[]{:S(2)}) collective-permute-start(f32[6,128,256]{2,1,0:T(8,128)} %get-tuple-element.909), channel_id=1, source_target_pairs={{0,1},{1,2},{2,3},{3,4},{4,5},{5,6},{6,7},{7,8},{8,9},{9,10},{10,1... | collective-permute-start | bytes 2359304 | tf_op jit(solution)/shard_map/while/body/eval_jaxpr/ppermute | solution.py:18
  988.9 116.0 %collective-permute-start.7 = (f32[6,256,128]{1,2,0:T(8,128)S(1)}, f32[6,256,128]{1,2,0:T(8,128)S(1)}, u32[]{:S(2)}, u32[]{:S(2)}) collective-permute-start(f32[6,256,128]{1,2,0:T(8,128)S(1)} %bitcast.313), channel_id=1, source_target_pairs={{1,0},{2,1},{3,2},{4,3},{5,4},{6,5},{7,6},{8,7},{9,8},{10,9},{11,1... | collective-permute-start | bytes 2359304 | tf_op jit(solution)/shard_map/while/body/eval_jaxpr/ppermute | solution.py:18
  992.7 121.3 %collective-permute-start.8 = (f32[6,128,256]{2,1,0:T(8,128)}, f32[6,128,256]{2,1,0:T(8,128)}, u32[]{:S(2)}, u32[]{:S(2)}) collective-permute-start(f32[6,128,256]{2,1,0:T(8,128)} %get-tuple-element.933), channel_id=1, source_target_pairs={{0,1},{1,2},{2,3},{3,4},{4,5},{5,6},{6,7},{7,8},{8,9},{9,10},{10,1... | collective-permute-start | bytes 2359304 | tf_op jit(solution)/shard_map/while/body/eval_jaxpr/ppermute | solution.py:18
  1047.1 53.3 %collective-permute-start.9 = (f32[2]{0:T(128)S(1)}, f32[2]{0:T(128)S(1)}, u32[]{:S(2)}, u32[]{:S(2)}) collective-permute-start(f32[2]{0:T(128)S(1)} %pad_maximum_fusion.14), channel_id=1, source_target_pairs={{0,1},{1,2},{2,3},{3,4},{4,5},{5,6},{6,7},{7,8},{8,9},{9,10},{10,1... | collective-permute-start | bytes 32 | tf_op jit(solution)/shard_map/while/body/eval_jaxpr/ppermute | solution.py:18
  1290.9 46.4 %collective-permute-start.2 = (f32[6,256,128]{1,2,0:T(8,128)S(1)}, f32[6,256,128]{1,2,0:T(8,128)S(1)}, u32[]{:S(2)}, u32[]{:S(2)}) collective-permute-start(f32[6,256,128]{1,2,0:T(8,128)S(1)} %bitcast.315), channel_id=1, source_target_pairs={{1,0},{2,1},{3,2},{4,3},{5,4},{6,5},{7,6},{8,7},{9,8},{10,9},{11,1... | collective-permute-start | bytes 2359304 | tf_op jit(solution)/shard_map/while/body/eval_jaxpr/ppermute | solution.py:18
  1294.8 55.3 %collective-permute-start.3 = (f32[6,128,256]{2,1,0:T(8,128)}, f32[6,128,256]{2,1,0:T(8,128)}, u32[]{:S(2)}, u32[]{:S(2)}) collective-permute-start(f32[6,128,256]{2,1,0:T(8,128)} %get-tuple-element.909), channel_id=1, source_target_pairs={{0,1},{1,2},{2,3},{3,4},{4,5},{5,6},{6,7},{7,8},{8,9},{9,10},{10,1... | collective-permute-start | bytes 2359304 | tf_op jit(solution)/shard_map/while/body/eval_jaxpr/ppermute | solution.py:18
  1530.0 114.8 %collective-permute-start.7 = (f32[6,256,128]{1,2,0:T(8,128)S(1)}, f32[6,256,128]{1,2,0:T(8,128)S(1)}, u32[]{:S(2)}, u32[]{:S(2)}) collective-permute-start(f32[6,256,128]{1,2,0:T(8,128)S(1)} %bitcast.313), channel_id=1, source_target_pairs={{1,0},{2,1},{3,2},{4,3},{5,4},{6,5},{7,6},{8,7},{9,8},{10,9},{11,1... | collective-permute-start | bytes 2359304 | tf_op jit(solution)/shard_map/while/body/eval_jaxpr/ppermute | solution.py:18
  1533.8 120.1 %collective-permute-start.8 = (f32[6,128,256]{2,1,0:T(8,128)}, f32[6,128,256]{2,1,0:T(8,128)}, u32[]{:S(2)}, u32[]{:S(2)}) collective-permute-start(f32[6,128,256]{2,1,0:T(8,128)} %get-tuple-element.933), channel_id=1, source_target_pairs={{0,1},{1,2},{2,3},{3,4},{4,5},{5,6},{6,7},{7,8},{8,9},{9,10},{10,1... | collective-permute-start | bytes 2359304 | tf_op jit(solution)/shard_map/while/body/eval_jaxpr/ppermute | solution.py:18
  1588.2 52.1 %collective-permute-start.9 = (f32[2]{0:T(128)S(1)}, f32[2]{0:T(128)S(1)}, u32[]{:S(2)}, u32[]{:S(2)}) collective-permute-start(f32[2]{0:T(128)S(1)} %pad_maximum_fusion.14), channel_id=1, source_target_pairs={{0,1},{1,2},{2,3},{3,4},{4,5},{5,6},{6,7},{7,8},{8,9},{9,10},{10,1... | collective-permute-start | bytes 32 | tf_op jit(solution)/shard_map/while/body/eval_jaxpr/ppermute | solution.py:18
  1831.1 46.4 %collective-permute-start.2 = (f32[6,256,128]{1,2,0:T(8,128)S(1)}, f32[6,256,128]{1,2,0:T(8,128)S(1)}, u32[]{:S(2)}, u32[]{:S(2)}) collective-permute-start(f32[6,256,128]{1,2,0:T(8,128)S(1)} %bitcast.315), channel_id=1, source_target_pairs={{1,0},{2,1},{3,2},{4,3},{5,4},{6,5},{7,6},{8,7},{9,8},{10,9},{11,1... | collective-permute-start | bytes 2359304 | tf_op jit(solution)/shard_map/while/body/eval_jaxpr/ppermute | solution.py:18
  1835.0 55.2 %collective-permute-start.3 = (f32[6,128,256]{2,1,0:T(8,128)}, f32[6,128,256]{2,1,0:T(8,128)}, u32[]{:S(2)}, u32[]{:S(2)}) collective-permute-start(f32[6,128,256]{2,1,0:T(8,128)} %get-tuple-element.909), channel_id=1, source_target_pairs={{0,1},{1,2},{2,3},{3,4},{4,5},{5,6},{6,7},{7,8},{8,9},{9,10},{10,1... | collective-permute-start | bytes 2359304 | tf_op jit(solution)/shard_map/while/body/eval_jaxpr/ppermute | solution.py:18
  2070.2 116.0 %collective-permute-start.7 = (f32[6,256,128]{1,2,0:T(8,128)S(1)}, f32[6,256,128]{1,2,0:T(8,128)S(1)}, u32[]{:S(2)}, u32[]{:S(2)}) collective-permute-start(f32[6,256,128]{1,2,0:T(8,128)S(1)} %bitcast.313), channel_id=1, source_target_pairs={{1,0},{2,1},{3,2},{4,3},{5,4},{6,5},{7,6},{8,7},{9,8},{10,9},{11,1... | collective-permute-start | bytes 2359304 | tf_op jit(solution)/shard_map/while/body/eval_jaxpr/ppermute | solution.py:18
  2074.1 121.3 %collective-permute-start.8 = (f32[6,128,256]{2,1,0:T(8,128)}, f32[6,128,256]{2,1,0:T(8,128)}, u32[]{:S(2)}, u32[]{:S(2)}) collective-permute-start(f32[6,128,256]{2,1,0:T(8,128)} %get-tuple-element.933), channel_id=1, source_target_pairs={{0,1},{1,2},{2,3},{3,4},{4,5},{5,6},{6,7},{7,8},{8,9},{9,10},{10,1... | collective-permute-start | bytes 2359304 | tf_op jit(solution)/shard_map/while/body/eval_jaxpr/ppermute | solution.py:18
  2128.4 53.3 %collective-permute-start.9 = (f32[2]{0:T(128)S(1)}, f32[2]{0:T(128)S(1)}, u32[]{:S(2)}, u32[]{:S(2)}) collective-permute-start(f32[2]{0:T(128)S(1)} %pad_maximum_fusion.14), channel_id=1, source_target_pairs={{0,1},{1,2},{2,3},{3,4},{4,5},{5,6},{6,7},{7,8},{8,9},{9,10},{10,1... | collective-permute-start | bytes 32 | tf_op jit(solution)/shard_map/while/body/eval_jaxpr/ppermute | solution.py:18
  (177 other events, 2020.1 us)
where the time goes:
time: 2210 us; the launch traced here: 2200 us
  other arithmetic  1150 us (52%)
  starting transfers between devices  399 us (18%)
  local copies, waits for them, and re-layouts  217 us (10%)
  blocking collectives  191 us (9%)
  matrix products  157 us (7%)
  loops' own time  47 us (2%)
  waiting for transfers between devices  42.3 us (2%)
    another operation x28, other arithmetic, split_sectors(): factor = jnp.linalg.cholesky(gram)  575 us
    another operation x20, other arithmetic, split_sectors(): jax.scipy.linalg.solve_triangular(factor, jnp.swapaxes(sample, 1, 2), low...  473 us
    ppermute x52, starting transfers between devices, shifted(): return lax.ppermute(value, axis, pairs)  398 us
    psum x4, blocking collectives, one_sweep(): summed = lax.psum((lost_now, log_now), 'site')  191 us
    dot_general x32, matrix products, product(): jnp.einsum('lam,lmb->lab', first, second, precision=lax.Precision.HIGHEST)  94.1 us
    another operation x1, loops' own time, body(): tensor, lost_sum, log_sum = lax.fori_loop(0, STEPS, one_step, start)  47 us
  transfers between devices with their start and end apart: 53, of which 20 were waited for; matrix products, arithmetic and copies ran while one was open for 8% of the time, Pallas kernels for 0%

commit v1 on v0

v1 whole, which is shorter than its diff:
```python
import functools

import jax
import jax.numpy as jnp
from jax import lax
from jax.experimental import pallas as pl
from jax.experimental.pallas import tpu as pltpu
from jax.sharding import PartitionSpec as P

STEPS = 4
HI = lax.Precision.HIGHEST


def mm(a, b, ca=1, cb=0):
    return lax.dot_general(
        a, b, (((ca,), (cb,)), ((), ())), precision=HI, preferred_element_type=jnp.float32
    )


def inverse_factors(w_ref, z_ref, n, width):
    strip = 32
    lanes = lax.broadcasted_iota(jnp.int32, (1, 8, width), 2)
    subs = lax.broadcasted_iota(jnp.int32, (1, 8, width), 1)
    for b in range(width // strip):
        r0 = b * strip
        groups = strip // 8
        ps = [w_ref[:, r0 + 8 * g : r0 + 8 * g + 8, :] for g in range(groups)]
        if b == 0:
            zs = [
                jnp.broadcast_to((lanes == subs + 8 * g).astype(jnp.float32), ps[0].shape)
                for g in range(groups)
            ]
        else:
            zs = [z_ref[:, r0 + 8 * g : r0 + 8 * g + 8, :] for g in range(groups)]
        for q in range(groups):
            vs = [
                [
                    jnp.broadcast_to(
                        ps[g][:, :, r0 + 8 * q + t : r0 + 8 * q + t + 1], ps[g].shape
                    )
                    if g >= q
                    else None
                    for g in range(groups)
                ]
                for t in range(8)
            ]
            for t in range(8):
                piv = vs[t][q][:, t : t + 1, :]
                inv = lax.rsqrt(piv)
                inv = inv * (1.5 - 0.5 * piv * inv * inv)
                inv2 = inv * inv

                def eliminate(rows):
                    pivot_row = rows[q][:, t : t + 1, :]
                    scaled = pivot_row * inv2
                    out = list(rows)
                    lower = rows[q] - vs[t][q] * scaled
                    out[q] = jnp.where(
                        subs > t, lower, jnp.where(subs == t, rows[q] * inv, rows[q])
                    )
                    for g in range(q + 1, groups):
                        out[g] = rows[g] - vs[t][g] * scaled
                    return out

                ps = eliminate(ps)
                zs = eliminate(zs)
                for t2 in range(t + 1, 8):
                    vs[t2] = eliminate(vs[t2])
        for g in range(groups):
            z_ref[:, r0 + 8 * g : r0 + 8 * g + 8, :] = zs[g]
            w_ref[:, r0 + 8 * g : r0 + 8 * g + 8, :] = ps[g]
        r1 = r0 + strip
        if r1 < width:
            rest = width - r1

            def trail(k, carry, r0=r0, r1=r1, rest=rest, b=b):
                pk = w_ref[k, r0:r1, :]
                zk = z_ref[k, r0:r1, :]
                both = mm(pk, jnp.concatenate([pk, zk], axis=1), 0, 0)[r1:]
                w_ref[k, r1:, :] = w_ref[k, r1:, :] - both[:, :width]
                if b == 0:
                    ri = lax.broadcasted_iota(jnp.int32, (rest, width), 0) + r1
                    ci = lax.broadcasted_iota(jnp.int32, (rest, width), 1)
                    old = (ri == ci).astype(jnp.float32)
                else:
                    old = z_ref[k, r1:, :]
                z_ref[k, r1:, :] = old - both[:, width:]
                return carry

            lax.fori_loop(0, n, trail, 0, unroll=True)


def sweep_kernel(
    n, width, flags, kept, gate,
    own, trav, ex_o, ex_t, sketch, acc,
    own_out, trav_out, ex2, ex3, acc_out,
    xl, xr, mat, smp, w_ref, z_ref, tot, wgt,
):
    full = 2 * n * width
    is_left = flags[0] == 1
    idle = flags[1] == 1

    prev_total = own[full : full + 1, :] + ex_o[2 * width : 2 * width + 1, :]
    prev_weight = own[full + 1 : full + 2, :] + ex_o[2 * width + 1 : 2 * width + 2, :]
    acc_out[...] = acc[...]
    acc_out[0:1, :] = acc[0:1, :] + (1.0 - prev_weight / prev_total)
    acc_out[1:2, :] = acc[1:2, :] + jnp.log(prev_total)
    other_weight = trav[full + 1 : full + 2, :] + ex_t[2 * width + 1 : 2 * width + 2, :]
    scale = 1.0 / jnp.sqrt(jnp.where(is_left, prev_weight, other_weight))

    for p in range(2):
        er = pl.ds(p * width, width)
        eo = ex_o[er, :]
        et = ex_t[er, :]
        xl[p, 0] = jnp.where(is_left, eo, et) * scale
        xr[p, n] = jnp.where(is_left, et, eo)
        for k in range(n):
            hr = pl.ds((p * n + k) * width, width)
            ho = own[hr, :]
            ht = trav[hr, :]
            xl[p, k + 1] = jnp.where(is_left, ho, ht) * scale
            xr[p, k] = jnp.where(is_left, ht, ho)

    def put(k, p, left_block, right_block):
        hr = pl.ds(pl.multiple_of((p * n + k) * width, width), width)
        own_out[hr, :] = jnp.where(is_left, left_block, right_block)
        trav_out[hr, :] = jnp.where(is_left, right_block, left_block)

    def stats(total, weight):
        rows = lax.broadcasted_iota(jnp.int32, (8, width), 0)
        tile = jnp.where(rows == 0, total, jnp.where(rows == 1, weight, 0.0))
        own_out[full : full + 8, :] = tile
        trav_out[full : full + 8, :] = tile
        ex2[2 * width : 2 * width + 8, :] = tile
        ex3[2 * width : 2 * width + 8, :] = tile

    @pl.when(idle)
    def _():
        for k in range(n):
            put(k, 0, xl[0, k + 1], xr[0, k])
            put(k, 1, xl[1, k], xr[1, k + 1])
        half = jnp.full((8, width), 0.5, jnp.float32)
        stats(half, half)

    @pl.when(jnp.logical_not(idle))
    def _():
        g = [gate[i] for i in range(6)]

        def mixes(j, carry):
            s01 = mm(xl[0, j], xr[1, j])
            s10 = mm(xl[1, j], xr[0, j])

            @pl.when(j > 0)
            def _():
                mat[jnp.maximum(j - 1, 0), :width, width:] = g[2] * s01 + g[3] * s10

            @pl.when(j < n)
            def _():
                mat[jnp.minimum(j, n - 1), width:, :width] = g[4] * s01 + g[5] * s10

            return carry

        lax.fori_loop(0, n + 1, mixes, 0, unroll=True)
        tot[...] = jnp.zeros_like(tot)
        wgt[...] = jnp.zeros_like(wgt)
        eye = (
            lax.broadcasted_iota(jnp.int32, (width, width), 0)
            == lax.broadcasted_iota(jnp.int32, (width, width), 1)
        )
        cols = lax.broadcasted_iota(jnp.int32, (1, width), 1)

        def first(k, carry):
            mat[k, :width, :width] = g[0] * mm(xl[0, k + 1], xr[0, k])
            mat[k, width:, width:] = g[1] * mm(xl[1, k], xr[1, k + 1])
            m = mat[k]
            sq = jnp.sum(m * m, axis=0, keepdims=True)
            tot[0:1, :] += sq[:, :width] + sq[:, width:]
            s = mm(m, sketch[k])
            smp[k] = s
            gram = mm(s, s, 0, 0)
            ds = jnp.sum(jnp.sum(s * s, axis=0, keepdims=True), axis=1, keepdims=True)
            kf = kept[k].astype(jnp.float32)
            ridge = 0.001 * ds / kf + 1e-06
            add = ridge + jnp.where(cols < kept[k], 0.0, 1.0)
            w_ref[k] = gram + jnp.where(eye, add, 0.0)
            return carry

        lax.fori_loop(0, n, first, 0, unroll=2)
        inverse_factors(w_ref, z_ref, n, width)

        def second(k, carry):
            basis = mm(smp[k], z_ref[k], 1, 1)
            red = mm(basis, mat[k], 0, 0)
            sq = jnp.sum(red * red, axis=0, keepdims=True)
            wgt[0:1, :] += sq[:, :width] + sq[:, width:]
            put(k, 0, basis[:width], red[:, :width])
            put(k, 1, basis[width:], red[:, width:])
            return carry

        lax.fori_loop(0, n, second, 0, unroll=2)
        t = jnp.sum(tot[0:1, :], axis=1, keepdims=True)
        wt = jnp.sum(wgt[0:1, :], axis=1, keepdims=True)
        stats(jnp.broadcast_to(t, (8, width)), jnp.broadcast_to(wt, (8, width)))

    for p in range(2):
        er = pl.ds(p * width, width)
        low = pl.ds(p * n * width, width)
        high = pl.ds((p * n + n - 1) * width, width)
        ex2[er, :] = jnp.where(is_left, trav_out[high, :], trav_out[low, :])
        ex3[er, :] = jnp.where(is_left, own_out[low, :], own_out[high, :])


def run_sweep(n, width, flags, kept, gate, own, trav, ex_o, ex_t, sketch, acc):
    f32 = jnp.float32
    big = jax.ShapeDtypeStruct((2 * n * width + 8, width), f32)
    small = jax.ShapeDtypeStruct((2 * width + 8, width), f32)
    smem = pl.BlockSpec(memory_space=pltpu.SMEM)
    vmem = pl.BlockSpec(memory_space=pltpu.VMEM)
    return pl.pallas_call(
        functools.partial(sweep_kernel, n, width),
        out_shape=(big, big, small, small, jax.ShapeDtypeStruct((8, width), f32)),
        in_specs=[smem] * 3 + [vmem] * 6,
        out_specs=(vmem,) * 5,
        scratch_shapes=[
            pltpu.VMEM((2, n + 1, width, width), f32),
            pltpu.VMEM((2, n + 1, width, width), f32),
            pltpu.VMEM((n, 2 * width, 2 * width), f32),
            pltpu.VMEM((n, 2 * width, width), f32),
            pltpu.VMEM((n, width, width), f32),
            pltpu.VMEM((n, width, width), f32),
            pltpu.VMEM((8, width), f32),
            pltpu.VMEM((8, width), f32),
        ],
        compiler_params=pltpu.CompilerParams(vmem_limit_bytes=40 * 1024 * 1024),
    )(flags, kept, gate, own, trav, ex_o, ex_t, sketch, acc)


def body(sites, sector_sizes, charge_steps, kept_counts, gates, sketches):
    f32 = jnp.float32
    chain = lax.axis_size("site")
    pos = lax.axis_index("site")
    count, width = sites.shape[2], sites.shape[-1]
    n = count // 2
    par = pos % 2
    odd = par == 1

    table = jnp.concatenate(
        [
            sector_sizes.astype(f32),
            kept_counts.astype(f32),
            charge_steps.astype(f32)[:, None],
            gates,
        ],
        axis=1,
    )
    table = lax.all_gather(table, "site", axis=0, tiled=True)
    steps = table[:, 2 * count].astype(jnp.int32)
    before = jnp.sum(jnp.where(jnp.arange(chain) < pos, steps, 0))
    step = charge_steps[0]
    prev = (pos + chain - 1) % chain
    following = lax.dynamic_index_in_dim(table, (pos + 1) % chain, 0, keepdims=False)[:count]
    prev_row = lax.dynamic_index_in_dim(table, prev, 0, keepdims=False)

    secs = jnp.arange(count, dtype=jnp.int32)
    mine = (secs[:n] + par * n)
    theirs = (secs[:n] + (1 - par) * n)
    order = jnp.concatenate(
        [
            mine,
            jnp.where(odd, 0, count - 1)[None].astype(jnp.int32),
            theirs,
            jnp.where(odd, n, n - 1)[None].astype(jnp.int32),
        ]
    )
    states = jnp.arange(width, dtype=jnp.int32)
    rows = states[None, :] < sector_sizes[0][:, None]
    pieces = []
    for p in range(2):
        label = (order - before - jnp.where(odd, p, 0)) % count
        target = (label + p - step) % count
        kr = rows[label]
        kc = states[None, :].astype(f32) < following[target][:, None]
        mask = kr[:, :, None] & kc[:, None, :]
        pieces.append(jnp.where(mask, sites[0, p][label], 0.0))
    both = jnp.stack(pieces)
    stat = jnp.where((jnp.arange(8) < 2)[:, None], 0.5, 0.0) * jnp.ones((1, width), f32)

    def flat(blocks):
        return jnp.concatenate([blocks.reshape(-1, width), stat], axis=0)

    own = flat(both[:, :n])
    ex_o = flat(both[:, n])
    even_pairs = [(i, i ^ 1) for i in range(chain)]
    odd_pairs = [
        (i, (i + 1) % chain if i % 2 == 1 else (i - 1) % chain) for i in range(chain)
    ]

    def perm(value, pairs):
        return lax.ppermute(value, "site", pairs)

    trav = perm(flat(both[:, n + 1 : 2 * n + 1]), even_pairs)
    ex_t = perm(flat(both[:, 2 * n + 1]), even_pairs)

    after = before + step
    own_sk = sketches[0][(mine - after) % count]
    send_sk = sketches[0][(theirs - after) % count]
    got_sk = perm(send_sk, [(i, (i + 1) % chain) for i in range(chain)])
    own_kept = kept_counts[0][(mine - after) % count]
    prev_kept = prev_row[count : 2 * count].astype(jnp.int32)[(mine - before) % count]
    own_sk = own_sk * (states[None, :] < own_kept[:, None]).astype(f32)[:, None, :]
    got_sk = got_sk * (states[None, :] < prev_kept[:, None]).astype(f32)[:, None, :]
    own_gate = gates[0]
    prev_gate = prev_row[2 * count + 1 :]
    sk, kp, gt, fl, moves, near, far = [], [], [], [], [], [], []
    for sweep in range(2):
        left = par == sweep
        sk.append(jnp.where(left, own_sk, got_sk))
        kp.append(jnp.where(left, own_kept, prev_kept))
        gt.append(jnp.where(left, own_gate, prev_gate))
        idle = (sweep == 1) & ((pos == 0) | (pos == chain - 1))
        fl.append(jnp.stack([left.astype(jnp.int32), idle.astype(jnp.int32)]))
        moves.append([(i, (i + (2 if i % 2 == sweep else -2)) % chain) for i in range(chain)])
        near.append(odd_pairs if sweep else even_pairs)
        far.append(even_pairs if sweep else odd_pairs)

    def call(sweep, own, trav, ex_o, ex_t, acc):
        return run_sweep(
            n, width, fl[sweep], kp[sweep], gt[sweep], own, trav, ex_o, ex_t, sk[sweep], acc
        )

    def one_sweep(sweep, carry):
        own, trav, ex2, ex3, acc = call(sweep, *carry)
        return (
            own, perm(trav, moves[sweep]), perm(ex2, near[sweep]), perm(ex3, far[sweep]), acc,
        )

    carry = one_sweep(0, (own, trav, ex_o, ex_t, jnp.zeros((8, width), f32)))

    def pair(index, carry):
        return one_sweep(0, one_sweep(1, carry))

    carry = lax.fori_loop(0, STEPS - 1, pair, carry)
    own, trav, _, _, acc = call(1, *carry)
    got = perm(trav, odd_pairs)
    full = 2 * n * width
    total = own[full, 0] + got[full, 0]
    weight = own[full + 1, 0] + got[full + 1, 0]
    sums = jnp.stack([acc[0, 0] + (1.0 - weight / total), acc[1, 0] + jnp.log(total)])
    sums = 0.5 * lax.psum(sums, "site")
    scale = jnp.where(odd, 1.0, 1.0 / jnp.sqrt(weight))
    halves = jnp.stack(
        [own[:full].reshape(2, n, width, width), got[:full].reshape(2, n, width, width)], axis=1
    ).reshape(2, count, width, width)
    out = []
    for p in range(2):
        charge = (secs + before + jnp.where(odd, p, 0)) % count
        out.append(halves[p][(charge + par * n) % count])
    return ((jnp.stack(out) * scale)[None], sums)


def solution(mesh):
    placed = (
        P("site", None, None, None, None),
        P("site", None),
        P("site"),
        P("site", None),
        P("site", None),
        P("site", None, None, None),
    )
    return jax.shard_map(
        body,
        mesh=mesh,
        in_specs=placed,
        out_specs=(P("site", None, None, None, None), P()),
        check_vma=False,
    )
```

time: 2210 us -> 497 us (0.22)
  other arithmetic: 1150 us -> 14.4 us
  starting transfers between devices: 399 us -> 119 us
  local copies, waits for them, and re-layouts: 217 us -> 17.2 us
  matrix products: 157 us -> 0 us
  Pallas kernels: 0 us -> 109 us
  blocking collectives: 191 us -> 108 us
  waiting for transfers between devices: 42.3 us -> 110 us
  loops' own time: 47 us -> 9.64 us
    another operation x65 -> x6, other arithmetic: 1070 us -> 1.4 us  [the longest x1 1.01 us: body(): jnp.stack([own[:full].reshape(2, n, width, width), got[:full].reshape(2,...]
    ppermute x53 -> x25, starting transfers between devices: 399 us -> 119 us  [perm(): return lax.ppermute(value, 'site', pairs)]
    gather x102 -> x12, local copies, waits for them, and re-layouts: 173 us -> 13 us  [the longest x2 3.21 us: body(): out.append(halves[p][(charge + par * n) % count])]
    dot_general x56 -> x0, matrix products: 150 us -> none  [the longest x32 94.1 us: product(): jnp.einsum('lam,lmb->lab', first, second, precision=lax.Precision.HIGHEST)]
    psum x4 -> x1, blocking collectives: 191 us -> 64.6 us  [body(): sums = 0.5 * lax.psum(sums, 'site')]
    pallas_call x0 -> x8, Pallas kernels: none -> 109 us  [run_sweep(): pl.pallas_call(functools.partial(sweep_kernel, n, width), out_shape=(big,...]
    ppermute x53 -> x25, waiting for transfers between devices: 42.3 us -> 110 us  [perm(): return lax.ppermute(value, 'site', pairs)]
    all_gather x0 -> x1, blocking collectives: none -> 43.3 us  [body(): table = lax.all_gather(table, 'site', axis=0, tiled=True)]
  transfers between devices with their start and end apart: 53 -> 25, of which waited for: 20 -> 17; matrix products, arithmetic and copies ran while one was open for 8% -> 2% of each run, Pallas kernels for 0% -> 0%
where the time goes in v1:
time: 497 us; the launch traced here: 493 us
  starting transfers between devices  119 us (24%)
  waiting for transfers between devices  110 us (22%)
  Pallas kernels  109 us (22%)
  blocking collectives  108 us (22%)
  local copies, waits for them, and re-layouts  17.2 us (3%)
  other arithmetic  14.4 us (3%)
  loops' own time  9.64 us (2%)
  between operations  6.38 us (1%)
    ppermute x25, starting transfers between devices, perm(): return lax.ppermute(value, 'site', pairs)  119 us
    ppermute x25, waiting for transfers between devices, perm(): return lax.ppermute(value, 'site', pairs)  110 us
    pallas_call x8, Pallas kernels, run_sweep(): pl.pallas_call(functools.partial(sweep_kernel, n, width), out_shape=(big,...  109 us
    psum x1, blocking collectives, body(): sums = 0.5 * lax.psum(sums, 'site')  64.6 us
    all_gather x1, blocking collectives, body(): table = lax.all_gather(table, 'site', axis=0, tiled=True)  43.3 us
  transfers between devices with their start and end apart: 25, of which 17 were waited for; matrix products, arithmetic and copies ran while one was open for 2% of the time, Pallas kernels for 0%

profile of v1, /device:TPU:0, one launch (start us, length us, event | category | flops | bytes accessed | tf_op | source)
XLA Modules:
  0.0 492.9 jit_solution(1877491082787641997)
XLA Ops:
  3.5 43.3 %all-gather = f32[32,1,31]{2,1,0:T(1,128)S(1)} all-gather(f32[1,1,31]{2,1,0:T(1,128)S(1)} %maximum_bitcast_fusion), channel_id=1, replica_groups=mesh['site'=32] {'site'}, dimensions={0}, use_global_device_ids=true | all-gather | bytes 4092 | tf_op jit(solution)/shard_map/all_gather | solution.py:256
  65.8 11.9 %collective-permute-done.8 = f32[6,256,128]{2,1,0:T(8,128)} collective-permute-done((f32[6,256,128]{2,1,0:T(8,128)}, f32[6,256,128]{2,1,0:T(8,128)}, u32[]{:S(2)}, u32[]{:S(2)}) %collective-permute-start.8) | collective-permute-done | bytes 786464 | tf_op jit(solution)/shard_map/ppermute | solution.py:299
  80.1 38.7 %shard_map.77 = (f32[1544,128]{1,0:T(8,128)}, f32[1544,128]{1,0:T(8,128)}, f32[264,128]{1,0:T(8,128)}, f32[264,128]{1,0:T(8,128)}, f32[8,128]{1,0:T(8,128)S(1)}) custom-call(s32[2]{0:T(128)S(1)} %add_convert_fusion.1.flags, s32[6]{0:T(128)S(1)} %get-tuple-element.298.kept, f32[6]{0:T(128)S(1)} %get-tuple-element.299.gate, ...), custom_call_target="tpu_custom_call" | custom-call | tf_op jit(solution)/shard_map/pallas_call | solution.py:219
  118.9 5.7 %collective-permute-start.11 = (f32[264,128]{1,0:T(8,128)}, f32[264,128]{1,0:T(8,128)}, u32[]{:S(2)}, u32[]{:S(2)}) collective-permute-start(f32[264,128]{1,0:T(8,128)} %get-tuple-element.99), channel_id=1, source_target_pairs={{0,31},{1,2},{2,1},{3,4},{4,3},{5,6},{6,5},{7,8},{8,7},{9,10},{10,... | collective-permute-start | bytes 405512 | tf_op jit(solution)/shard_map/ppermute | solution.py:299
  128.9 7.1 %collective-permute-done.9 = f32[1544,128]{1,0:T(8,128)S(1)} collective-permute-done((f32[1544,128]{1,0:T(8,128)}, f32[1544,128]{1,0:T(8,128)S(1)}, u32[]{:S(2)}, u32[]{:S(2)}) %collective-permute-start.9) | collective-permute-done | bytes 790560 | tf_op jit(solution)/shard_map/ppermute | solution.py:299
  136.0 262.8 %while.18 = (s32[]{:T(128)}, f32[1544,128]{1,0:T(8,128)}, f32[1544,128]{1,0:T(8,128)S(1)}, f32[264,128]{1,0:T(8,128)}, f32[264,128]{1,0:T(8,128)}, /*index=5*/f3...) while((s32[]{:T(128)}, f32[1544,128]{1,0:T(8,128)}, ...), condition=%wide.region_2.3_spmd, body=%wide.region_1.2_spmd.sunk | while | flops 2 | bytes 11633049 | solution.py:342
  137.8 18.7 %collective-permute-start = (f32[1544,128]{1,0:T(8,128)S(1)}, f32[1544,128]{1,0:T(8,128)S(1)}, u32[]{:S(2)}, u32[]{:S(2)}) collective-permute-start(f32[1544,128]{1,0:T(8,128)S(1)} %get-tuple-element.278), channel_id=1, source_target_pairs={{0,30},{1,3},{2,0},{3,5},{4,2},{5,7},{6,4},{7,9},{8,6},{9,11},{10,... | collective-permute-start | bytes 2371592 | tf_op jit(solution)/shard_map/while/body/eval_jaxpr/ppermute | solution.py:299
  161.8 11.3 %collective-permute-done.1.ex_o = f32[264,128]{1,0:T(8,128)S(1)} collective-permute-done((f32[264,128]{1,0:T(8,128)S(1)}, f32[264,128]{1,0:T(8,128)S(1)}, u32[]{:S(2)}, u32[]{:S(2)}) %collective-permute-start.1) | collective-permute-done | bytes 135200 | tf_op jit(solution)/shard_map/while/body/eval_jaxpr/ppermute | solution.py:299
  174.8 20.7 %eval_jaxpr.3 = (f32[1544,128]{1,0:T(8,128)}, f32[1544,128]{1,0:T(8,128)S(1)}, f32[264,128]{1,0:T(8,128)S(1)}, f32[264,128]{1,0:T(8,128)S(1)}, f32[8,128]{1,0:T(8,128)S(1)}) custom-call(s32[2]{0:T(128)S(1)} %get-tuple-element.327.flags, s32[6]{0:T(128)S(1)} %get-tuple-element.328.kept, f32[6]{0:T(128)S(1)} %get-tuple-element.329.gate, ...), custom_call_target="tpu_custom_call" | custom-call | tf_op jit(solution)/shard_map/while/body/eval_jaxpr/pallas_call | solution.py:219
  201.7 8.2 %collective-permute-done.5 = f32[264,128]{1,0:T(8,128)} collective-permute-done((f32[264,128]{1,0:T(8,128)S(1)}, f32[264,128]{1,0:T(8,128)}, u32[]{:S(2)}, u32[]{:S(2)}) %collective-permute-start.5) | collective-permute-done | bytes 135200 | tf_op jit(solution)/shard_map/while/body/eval_jaxpr/ppermute | solution.py:299
  214.6 30.6 %collective-permute-start = (f32[1544,128]{1,0:T(8,128)S(1)}, f32[1544,128]{1,0:T(8,128)S(1)}, u32[]{:S(2)}, u32[]{:S(2)}) collective-permute-start(f32[1544,128]{1,0:T(8,128)S(1)} %get-tuple-element.278), channel_id=1, source_target_pairs={{0,30},{1,3},{2,0},{3,5},{4,2},{5,7},{6,4},{7,9},{8,6},{9,11},{10,... | collective-permute-start | bytes 2371592 | tf_op jit(solution)/shard_map/while/body/eval_jaxpr/ppermute | solution.py:299
  246.1 11.3 %collective-permute-done.1.ex_o = f32[264,128]{1,0:T(8,128)S(1)} collective-permute-done((f32[264,128]{1,0:T(8,128)S(1)}, f32[264,128]{1,0:T(8,128)S(1)}, u32[]{:S(2)}, u32[]{:S(2)}) %collective-permute-start.1) | collective-permute-done | bytes 135200 | tf_op jit(solution)/shard_map/while/body/eval_jaxpr/ppermute | solution.py:299
  257.4 20.7 %eval_jaxpr.3 = (f32[1544,128]{1,0:T(8,128)}, f32[1544,128]{1,0:T(8,128)S(1)}, f32[264,128]{1,0:T(8,128)S(1)}, f32[264,128]{1,0:T(8,128)S(1)}, f32[8,128]{1,0:T(8,128)S(1)}) custom-call(s32[2]{0:T(128)S(1)} %get-tuple-element.327.flags, s32[6]{0:T(128)S(1)} %get-tuple-element.328.kept, f32[6]{0:T(128)S(1)} %get-tuple-element.329.gate, ...), custom_call_target="tpu_custom_call" | custom-call | tf_op jit(solution)/shard_map/while/body/eval_jaxpr/pallas_call | solution.py:219
  278.1 8.9 %collective-permute-start.3 = (f32[1544,128]{1,0:T(8,128)S(1)}, f32[1544,128]{1,0:T(8,128)S(1)}, u32[]{:S(2)}, u32[]{:S(2)}) collective-permute-start(f32[1544,128]{1,0:T(8,128)S(1)} %get-tuple-element.283), channel_id=1, source_target_pairs={{0,2},{1,31},{2,4},{3,1},{4,6},{5,3},{6,8},{7,5},{8,10},{9,7},{10,... | collective-permute-start | bytes 2371592 | tf_op jit(solution)/shard_map/while/body/eval_jaxpr/ppermute | solution.py:299
  288.5 8.2 %collective-permute-done.5 = f32[264,128]{1,0:T(8,128)} collective-permute-done((f32[264,128]{1,0:T(8,128)S(1)}, f32[264,128]{1,0:T(8,128)}, u32[]{:S(2)}, u32[]{:S(2)}) %collective-permute-start.5) | collective-permute-done | bytes 135200 | tf_op jit(solution)/shard_map/while/body/eval_jaxpr/ppermute | solution.py:299
  296.7 7.7 %collective-permute-done.3 = f32[1544,128]{1,0:T(8,128)S(1)} collective-permute-done((f32[1544,128]{1,0:T(8,128)S(1)}, f32[1544,128]{1,0:T(8,128)S(1)}, u32[]{:S(2)}, u32[]{:S(2)}) %collective-permute-start.3) | collective-permute-done | bytes 790560 | tf_op jit(solution)/shard_map/while/body/eval_jaxpr/ppermute | solution.py:299
  306.3 24.1 %collective-permute-start = (f32[1544,128]{1,0:T(8,128)S(1)}, f32[1544,128]{1,0:T(8,128)S(1)}, u32[]{:S(2)}, u32[]{:S(2)}) collective-permute-start(f32[1544,128]{1,0:T(8,128)S(1)} %get-tuple-element.278), channel_id=1, source_target_pairs={{0,30},{1,3},{2,0},{3,5},{4,2},{5,7},{6,4},{7,9},{8,6},{9,11},{10,... | collective-permute-start | bytes 2371592 | tf_op jit(solution)/shard_map/while/body/eval_jaxpr/ppermute | solution.py:299
  332.9 11.3 %collective-permute-done.1.ex_o = f32[264,128]{1,0:T(8,128)S(1)} collective-permute-done((f32[264,128]{1,0:T(8,128)S(1)}, f32[264,128]{1,0:T(8,128)S(1)}, u32[]{:S(2)}, u32[]{:S(2)}) %collective-permute-start.1) | collective-permute-done | bytes 135200 | tf_op jit(solution)/shard_map/while/body/eval_jaxpr/ppermute | solution.py:299
  344.4 20.7 %eval_jaxpr.3 = (f32[1544,128]{1,0:T(8,128)}, f32[1544,128]{1,0:T(8,128)S(1)}, f32[264,128]{1,0:T(8,128)S(1)}, f32[264,128]{1,0:T(8,128)S(1)}, f32[8,128]{1,0:T(8,128)S(1)}) custom-call(s32[2]{0:T(128)S(1)} %get-tuple-element.327.flags, s32[6]{0:T(128)S(1)} %get-tuple-element.328.kept, f32[6]{0:T(128)S(1)} %get-tuple-element.329.gate, ...), custom_call_target="tpu_custom_call" | custom-call | tf_op jit(solution)/shard_map/while/body/eval_jaxpr/pallas_call | solution.py:219
  365.1 7.6 %collective-permute-start.3 = (f32[1544,128]{1,0:T(8,128)S(1)}, f32[1544,128]{1,0:T(8,128)S(1)}, u32[]{:S(2)}, u32[]{:S(2)}) collective-permute-start(f32[1544,128]{1,0:T(8,128)S(1)} %get-tuple-element.283), channel_id=1, source_target_pairs={{0,2},{1,31},{2,4},{3,1},{4,6},{5,3},{6,8},{7,5},{8,10},{9,7},{10,... | collective-permute-start | bytes 2371592 | tf_op jit(solution)/shard_map/while/body/eval_jaxpr/ppermute | solution.py:299
  374.2 8.2 %collective-permute-done.5 = f32[264,128]{1,0:T(8,128)} collective-permute-done((f32[264,128]{1,0:T(8,128)S(1)}, f32[264,128]{1,0:T(8,128)}, u32[]{:S(2)}, u32[]{:S(2)}) %collective-permute-start.5) | collective-permute-done | bytes 135200 | tf_op jit(solution)/shard_map/while/body/eval_jaxpr/ppermute | solution.py:299
  382.4 6.8 %collective-permute-done.3 = f32[1544,128]{1,0:T(8,128)S(1)} collective-permute-done((f32[1544,128]{1,0:T(8,128)S(1)}, f32[1544,128]{1,0:T(8,128)S(1)}, u32[]{:S(2)}, u32[]{:S(2)}) %collective-permute-start.3) | collective-permute-done | bytes 790560 | tf_op jit(solution)/shard_map/while/body/eval_jaxpr/ppermute | solution.py:299
  408.2 8.1 %collective-permute-done.12 = f32[1544,128]{1,0:T(8,128)S(1)} collective-permute-done((f32[1544,128]{1,0:T(8,128)S(1)}, f32[1544,128]{1,0:T(8,128)S(1)}, u32[]{:S(2)}, u32[]{:S(2)}) %collective-permute-start.12) | collective-permute-done | bytes 790560 | tf_op jit(solution)/shard_map/ppermute | solution.py:299
  420.9 64.6 %psum.7 = f32[2]{0:T(128)S(1)} all-reduce(f32[2]{0:T(128)S(1)} %pad_maximum_fusion.6), channel_id=1, replica_groups=mesh['site'=32] {'site'}, use_global_device_ids=true, to_apply=%region_3.4 | all-reduce | flops 2 | bytes 16 | tf_op jit(solution)/shard_map/psum | solution.py:349
  (118 shorter events, 72.6 us)
Async XLA Ops:
  59.2 20.9 %collective-permute-start.7 = (f32[264,128]{1,0:T(8,128)}, f32[264,128]{1,0:T(8,128)S(1)}, u32[]{:S(2)}, u32[]{:S(2)}) collective-permute-start(f32[264,128]{1,0:T(8,128)} %get-tuple-element.158), channel_id=1, source_target_pairs={{0,1},{1,0},{2,3},{3,2},{4,5},{5,4},{6,7},{7,6},{8,9},{9,8},{10,11... | collective-permute-start | bytes 405512 | tf_op jit(solution)/shard_map/ppermute | solution.py:299
  60.7 19.4 %collective-permute-start.6 = (f32[1544,128]{1,0:T(8,128)}, f32[1544,128]{1,0:T(8,128)S(1)}, u32[]{:S(2)}, u32[]{:S(2)}) collective-permute-start(f32[1544,128]{1,0:T(8,128)} %get-tuple-element.160), channel_id=1, source_target_pairs={{0,1},{1,0},{2,3},{3,2},{4,5},{5,4},{6,7},{7,6},{8,9},{9,8},{10,11... | collective-permute-start | bytes 2371592 | tf_op jit(solution)/shard_map/ppermute | solution.py:299
  62.4 15.3 %collective-permute-start.8 = (f32[6,256,128]{2,1,0:T(8,128)}, f32[6,256,128]{2,1,0:T(8,128)}, u32[]{:S(2)}, u32[]{:S(2)}) collective-permute-start(f32[6,256,128]{2,1,0:T(8,128)} %gather_fusion.9), channel_id=1, source_target_pairs={{0,1},{1,2},{2,3},{3,4},{4,5},{5,6},{6,7},{7,8},{8,9},{9,10},{10,1... | collective-permute-start | bytes 2359304 | tf_op jit(solution)/shard_map/ppermute | solution.py:299
  118.9 17.1 %collective-permute-start.9 = (f32[1544,128]{1,0:T(8,128)}, f32[1544,128]{1,0:T(8,128)S(1)}, u32[]{:S(2)}, u32[]{:S(2)}) collective-permute-start(f32[1544,128]{1,0:T(8,128)} %get-tuple-element.97), channel_id=1, source_target_pairs={{0,2},{1,31},{2,4},{3,1},{4,6},{5,3},{6,8},{7,5},{8,10},{9,7},{10,... | collective-permute-start | bytes 2371592 | tf_op jit(solution)/shard_map/ppermute | solution.py:299
  118.9 5.8 %collective-permute-start.10 = (f32[264,128]{1,0:T(8,128)}, f32[264,128]{1,0:T(8,128)}, u32[]{:S(2)}, u32[]{:S(2)}) collective-permute-start(f32[264,128]{1,0:T(8,128)} %get-tuple-element.98), channel_id=1, source_target_pairs={{0,1},{1,0},{2,3},{3,2},{4,5},{5,4},{6,7},{7,6},{8,9},{9,8},{10,11... | collective-permute-start | bytes 405512 | tf_op jit(solution)/shard_map/ppermute | solution.py:299
  118.9 9.9 %collective-permute-start.11 = (f32[264,128]{1,0:T(8,128)}, f32[264,128]{1,0:T(8,128)}, u32[]{:S(2)}, u32[]{:S(2)}) collective-permute-start(f32[264,128]{1,0:T(8,128)} %get-tuple-element.99), channel_id=1, source_target_pairs={{0,31},{1,2},{2,1},{3,4},{4,3},{5,6},{6,5},{7,8},{8,7},{9,10},{10,... | collective-permute-start | bytes 405512 | tf_op jit(solution)/shard_map/ppermute | solution.py:299
  137.8 37.0 %collective-permute-start = (f32[1544,128]{1,0:T(8,128)S(1)}, f32[1544,128]{1,0:T(8,128)S(1)}, u32[]{:S(2)}, u32[]{:S(2)}) collective-permute-start(f32[1544,128]{1,0:T(8,128)S(1)} %get-tuple-element.278), channel_id=1, source_target_pairs={{0,30},{1,3},{2,0},{3,5},{4,2},{5,7},{6,4},{7,9},{8,6},{9,11},{10,... | collective-permute-start | bytes 2371592 | tf_op jit(solution)/shard_map/while/body/eval_jaxpr/ppermute | solution.py:299
  156.5 16.5 %collective-permute-start.1 = (f32[264,128]{1,0:T(8,128)S(1)}, f32[264,128]{1,0:T(8,128)S(1)}, u32[]{:S(2)}, u32[]{:S(2)}) collective-permute-start(f32[264,128]{1,0:T(8,128)S(1)} %get-tuple-element.279), channel_id=1, source_target_pairs={{0,31},{1,2},{2,1},{3,4},{4,3},{5,6},{6,5},{7,8},{8,7},{9,10},{10,... | collective-permute-start | bytes 405512 | tf_op jit(solution)/shard_map/while/body/eval_jaxpr/ppermute | solution.py:299
  161.7 11.3 %collective-permute-start.2 = (f32[264,128]{1,0:T(8,128)S(1)}, f32[264,128]{1,0:T(8,128)S(1)}, u32[]{:S(2)}, u32[]{:S(2)}) collective-permute-start(f32[264,128]{1,0:T(8,128)S(1)} %get-tuple-element.280), channel_id=1, source_target_pairs={{0,1},{1,0},{2,3},{3,2},{4,5},{5,4},{6,7},{7,6},{8,9},{9,8},{10,11... | collective-permute-start | bytes 405512 | tf_op jit(solution)/shard_map/while/body/eval_jaxpr/ppermute | solution.py:299
  195.5 17.2 %collective-permute-start.3 = (f32[1544,128]{1,0:T(8,128)S(1)}, f32[1544,128]{1,0:T(8,128)S(1)}, u32[]{:S(2)}, u32[]{:S(2)}) collective-permute-start(f32[1544,128]{1,0:T(8,128)S(1)} %get-tuple-element.283), channel_id=1, source_target_pairs={{0,2},{1,31},{2,4},{3,1},{4,6},{5,3},{6,8},{7,5},{8,10},{9,7},{10,... | collective-permute-start | bytes 2371592 | tf_op jit(solution)/shard_map/while/body/eval_jaxpr/ppermute | solution.py:299
  200.2 1.5 collective-permute-start.4
  200.2 9.7 %collective-permute-start.5 = (f32[264,128]{1,0:T(8,128)S(1)}, f32[264,128]{1,0:T(8,128)}, u32[]{:S(2)}, u32[]{:S(2)}) collective-permute-start(f32[264,128]{1,0:T(8,128)S(1)} %get-tuple-element.285), channel_id=1, source_target_pairs={{0,31},{1,2},{2,1},{3,4},{4,3},{5,6},{6,5},{7,8},{8,7},{9,10},{10,... | collective-permute-start | bytes 405512 | tf_op jit(solution)/shard_map/while/body/eval_jaxpr/ppermute | solution.py:299
  214.6 42.8 %collective-permute-start = (f32[1544,128]{1,0:T(8,128)S(1)}, f32[1544,128]{1,0:T(8,128)S(1)}, u32[]{:S(2)}, u32[]{:S(2)}) collective-permute-start(f32[1544,128]{1,0:T(8,128)S(1)} %get-tuple-element.278), channel_id=1, source_target_pairs={{0,30},{1,3},{2,0},{3,5},{4,2},{5,7},{6,4},{7,9},{8,6},{9,11},{10,... | collective-permute-start | bytes 2371592 | tf_op jit(solution)/shard_map/while/body/eval_jaxpr/ppermute | solution.py:299
  245.2 12.2 %collective-permute-start.1 = (f32[264,128]{1,0:T(8,128)S(1)}, f32[264,128]{1,0:T(8,128)S(1)}, u32[]{:S(2)}, u32[]{:S(2)}) collective-permute-start(f32[264,128]{1,0:T(8,128)S(1)} %get-tuple-element.279), channel_id=1, source_target_pairs={{0,31},{1,2},{2,1},{3,4},{4,3},{5,6},{6,5},{7,8},{8,7},{9,10},{10,... | collective-permute-start | bytes 405512 | tf_op jit(solution)/shard_map/while/body/eval_jaxpr/ppermute | solution.py:299
  246.1 11.3 %collective-permute-start.2 = (f32[264,128]{1,0:T(8,128)S(1)}, f32[264,128]{1,0:T(8,128)S(1)}, u32[]{:S(2)}, u32[]{:S(2)}) collective-permute-start(f32[264,128]{1,0:T(8,128)S(1)} %get-tuple-element.280), channel_id=1, source_target_pairs={{0,1},{1,0},{2,3},{3,2},{4,5},{5,4},{6,7},{7,6},{8,9},{9,8},{10,11... | collective-permute-start | bytes 405512 | tf_op jit(solution)/shard_map/while/body/eval_jaxpr/ppermute | solution.py:299
  278.1 26.4 %collective-permute-start.3 = (f32[1544,128]{1,0:T(8,128)S(1)}, f32[1544,128]{1,0:T(8,128)S(1)}, u32[]{:S(2)}, u32[]{:S(2)}) collective-permute-start(f32[1544,128]{1,0:T(8,128)S(1)} %get-tuple-element.283), channel_id=1, source_target_pairs={{0,2},{1,31},{2,4},{3,1},{4,6},{5,3},{6,8},{7,5},{8,10},{9,7},{10,... | collective-permute-start | bytes 2371592 | tf_op jit(solution)/shard_map/while/body/eval_jaxpr/ppermute | solution.py:299
  287.0 1.5 collective-permute-start.4
  287.0 9.7 %collective-permute-start.5 = (f32[264,128]{1,0:T(8,128)S(1)}, f32[264,128]{1,0:T(8,128)}, u32[]{:S(2)}, u32[]{:S(2)}) collective-permute-start(f32[264,128]{1,0:T(8,128)S(1)} %get-tuple-element.285), channel_id=1, source_target_pairs={{0,31},{1,2},{2,1},{3,4},{4,3},{5,6},{6,5},{7,8},{8,7},{9,10},{10,... | collective-permute-start | bytes 405512 | tf_op jit(solution)/shard_map/while/body/eval_jaxpr/ppermute | solution.py:299
  306.3 38.1 %collective-permute-start = (f32[1544,128]{1,0:T(8,128)S(1)}, f32[1544,128]{1,0:T(8,128)S(1)}, u32[]{:S(2)}, u32[]{:S(2)}) collective-permute-start(f32[1544,128]{1,0:T(8,128)S(1)} %get-tuple-element.278), channel_id=1, source_target_pairs={{0,30},{1,3},{2,0},{3,5},{4,2},{5,7},{6,4},{7,9},{8,6},{9,11},{10,... | collective-permute-start | bytes 2371592 | tf_op jit(solution)/shard_map/while/body/eval_jaxpr/ppermute | solution.py:299
  330.4 13.8 %collective-permute-start.1 = (f32[264,128]{1,0:T(8,128)S(1)}, f32[264,128]{1,0:T(8,128)S(1)}, u32[]{:S(2)}, u32[]{:S(2)}) collective-permute-start(f32[264,128]{1,0:T(8,128)S(1)} %get-tuple-element.279), channel_id=1, source_target_pairs={{0,31},{1,2},{2,1},{3,4},{4,3},{5,6},{6,5},{7,8},{8,7},{9,10},{10,... | collective-permute-start | bytes 405512 | tf_op jit(solution)/shard_map/while/body/eval_jaxpr/ppermute | solution.py:299
  332.9 11.3 %collective-permute-start.2 = (f32[264,128]{1,0:T(8,128)S(1)}, f32[264,128]{1,0:T(8,128)S(1)}, u32[]{:S(2)}, u32[]{:S(2)}) collective-permute-start(f32[264,128]{1,0:T(8,128)S(1)} %get-tuple-element.280), channel_id=1, source_target_pairs={{0,1},{1,0},{2,3},{3,2},{4,5},{5,4},{6,7},{7,6},{8,9},{9,8},{10,11... | collective-permute-start | bytes 405512 | tf_op jit(solution)/shard_map/while/body/eval_jaxpr/ppermute | solution.py:299
  365.1 24.1 %collective-permute-start.3 = (f32[1544,128]{1,0:T(8,128)S(1)}, f32[1544,128]{1,0:T(8,128)S(1)}, u32[]{:S(2)}, u32[]{:S(2)}) collective-permute-start(f32[1544,128]{1,0:T(8,128)S(1)} %get-tuple-element.283), channel_id=1, source_target_pairs={{0,2},{1,31},{2,4},{3,1},{4,6},{5,3},{6,8},{7,5},{8,10},{9,7},{10,... | collective-permute-start | bytes 2371592 | tf_op jit(solution)/shard_map/while/body/eval_jaxpr/ppermute | solution.py:299
  372.7 9.7 %collective-permute-start.5 = (f32[264,128]{1,0:T(8,128)S(1)}, f32[264,128]{1,0:T(8,128)}, u32[]{:S(2)}, u32[]{:S(2)}) collective-permute-start(f32[264,128]{1,0:T(8,128)S(1)} %get-tuple-element.285), channel_id=1, source_target_pairs={{0,31},{1,2},{2,1},{3,4},{4,3},{5,6},{6,5},{7,8},{8,7},{9,10},{10,... | collective-permute-start | bytes 405512 | tf_op jit(solution)/shard_map/while/body/eval_jaxpr/ppermute | solution.py:299
  401.3 15.1 %collective-permute-start.12 = (f32[1544,128]{1,0:T(8,128)S(1)}, f32[1544,128]{1,0:T(8,128)S(1)}, u32[]{:S(2)}, u32[]{:S(2)}) collective-permute-start(f32[1544,128]{1,0:T(8,128)S(1)} %get-tuple-element.107), channel_id=1, source_target_pairs={{0,31},{1,2},{2,1},{3,4},{4,3},{5,6},{6,5},{7,8},{8,7},{9,10},{10,... | collective-permute-start | bytes 2371592 | tf_op jit(solution)/shard_map/ppermute | solution.py:299
  (11 other events, 235.5 us)
